TPU v7x, 512 devices: a whole 4x8x8 slice. The times are simulated.
512 devices in a mesh: rep: 32 (over z, y_hi), sp: 16 (over y_lo, x, core).
Axes of the slice: x: 4, y: 8 (y_hi: 4, y_lo: 2; y = y_hi * 2 + y_lo), z: 8, core: 2. Of those that a mesh axis runs over, the one named last changes fastest.
Arguments:
- queries: bfloat16 [32, 3072, 2048], P('rep', 'sp'), may hold values from -13 to 13
- key_rows: bfloat16 [32, 3072, 2048], P('rep', 'sp'), may hold values from -13 to 13
- values: bfloat16 [32, 3072, 2048], P('rep', 'sp'), may hold values from -6 to 6
- out_grad: bfloat16 [32, 3072, 3072], P('rep', 'sp'), may hold values from -6 to 6
- clip_count: int32 [32], P('rep'), may hold values from 1 to 3, as said below
- clip_lengths: int32 [32, 3], P('rep'), may hold values from 0 to 3072, as said below
- adapter_in: float32 [2048, 128], P('sp'), may hold values from -4 to 4
- adapter_out: float32 [128, 3072], P('sp'), may hold values from -4 to 4
- moment_in: float32 [2048, 128], P('sp'), may hold values from -3 to 3
- square_in: float32 [2048, 128], P('sp'), may hold values from 0.05 to 2
- moment_out: float32 [128, 3072], P('sp'), may hold values from -3 to 3
- square_out: float32 [128, 3072], P('sp'), may hold values from 0.05 to 2
Outputs:
- momentum_in: float32 [2048, 128], P('sp')
- variance_in: float32 [2048, 128], P('sp')
- update_in: float32 [2048, 128], P('sp')
- momentum_out: float32 [128, 3072], P('sp')
- variance_out: float32 [128, 3072], P('sp')
- update_out: float32 [128, 3072], P('sp')
Inputs may be any that keep to these rules, and one draw needn't show every extreme that they name: `clip_count`: in every draw some replica has 1 clip and some replica has 3. `clip_lengths`: each entry is a multiple of 384; entries at or beyond a replica's clip count are 0, the others 384 or more; the entries of a replica sum to at most 3072, and in every draw some replica holds a single clip of exactly 3072.
All inputs are finite; a program needn't handle non-finite values.
Results may differ from a plain program's by a relative error of at most 0.0017.
Values may be sent and summed in bfloat16 or wider, within the bound.
A program may use at most 64 MiB of HBM per device.

v0:
```python
import math
import jax
import jax.numpy as jnp
from jax import lax
from jax.sharding import PartitionSpec as P

HD = 128
MAX_CLIPS = 3
first_rate = 0.9
second_rate = 0.999
adam_steps = 100.0
adam_epsilon = 1e-08
decay_rate = 0.1


def laid_out(blocks, dim):
    shape = list(blocks.shape[1:])
    shape[dim] *= blocks.shape[0]
    return jnp.moveaxis(blocks, 0, dim).reshape(shape)


def gather_packed(arrays, axis, dims):
    ravelled = jnp.concatenate([a.reshape(-1) for a in arrays])
    lines, at, done = (lax.all_gather(ravelled, axis), 0, [])
    for a, dim in zip(arrays, dims):
        blocks = lines[:, at : at + a.size].reshape(-1, *a.shape)
        done.append(laid_out(blocks, dim))
        at += a.size
    return tuple(done)


def cut_along(array, dim, peers):
    shape = array.shape
    blocks = array.reshape(*shape[:dim], peers, shape[dim] // peers, *shape[dim + 1 :])
    return jnp.moveaxis(blocks, dim, 0)


def sum_packed(arrays, axis, dims):
    peers = lax.axis_size(axis)
    blocks = [cut_along(a, dim, peers) for a, dim in zip(arrays, dims)]
    lines = jnp.concatenate([b.reshape(peers, -1) for b in blocks], axis=1)
    extent = max(16, -(-lines.shape[1] // 1024) * 8)
    lines = jnp.pad(lines, ((0, 0), (0, extent * 128 - lines.shape[1]))).reshape(-1, 128)
    ravelled, at, done = (lax.psum_scatter(lines, axis, tiled=True).reshape(-1), 0, [])
    for b in blocks:
        part = b[0]
        done.append(ravelled[at : at + part.size].reshape(part.shape))
        at += part.size
    return tuple(done)


def padded_to(lines, peers):
    spare = -lines.shape[0] % peers
    if not spare:
        return lines
    return jnp.concatenate([lines, jnp.zeros((spare, *lines.shape[1:]), lines.dtype)])


def sent_to_all(array, axis):
    peers = lax.axis_size(axis)
    return lax.all_to_all(
        jnp.broadcast_to(array[None], (peers, *array.shape)), axis, 0, 0, tiled=True
    )


def gathered_copies(array, axis, dim):
    return laid_out(sent_to_all(array, axis), dim)


def summed_on_arrival(array, axis, dim):
    blocks = cut_along(array, dim, lax.axis_size(axis))
    arrived = lax.all_to_all(blocks, axis, split_axis=0, concat_axis=0, tiled=True)
    return arrived.sum(axis=0)


def total_of(array, axes):
    padded = padded_to(array, lax.axis_size(axes))
    whole = gathered_copies(summed_on_arrival(padded, axes, 0), axes, 0)
    return lax.slice_in_dim(whole, 0, len(array)).reshape(array.shape)


def packed_total(arrays, axis):
    ends = [0]
    for a in arrays:
        ends.append(ends[-1] + a.size)
    total = total_of(jnp.concatenate([a.ravel() for a in arrays]), axis)
    return tuple((total[b:e].reshape(a.shape) for a, b, e in zip(arrays, ends, ends[1:])))


def segment_ids(count, lengths, positions):
    active = (jnp.arange(lengths.shape[0], dtype=jnp.int32) < count).astype(lengths.dtype)
    ends = jnp.cumsum(lengths * active)
    return jnp.sum((positions[:, None] >= ends[None, :]).astype(jnp.int32), axis=1)


def adamw(param, grad, moment, square):
    momentum = first_rate * moment + (1.0 - first_rate) * grad
    variance = second_rate * square + (1.0 - second_rate) * grad * grad
    first_hat = momentum / (1.0 - first_rate**adam_steps)
    second_hat = variance / (1.0 - second_rate**adam_steps)
    update = first_hat / (jnp.sqrt(second_hat) + adam_epsilon) + decay_rate * param
    return (momentum, variance, update)


def contract_rows(left, right):
    return lax.dot_general(
        left, right, (((0,), (0,)), ((), ())), preferred_element_type=jnp.float32
    )


def per_device(
    queries,
    key_rows,
    values,
    out_grad,
    clip_count,
    clip_lengths,
    adapter_in,
    adapter_out,
    moment_in,
    square_in,
    moment_out,
    square_out,
):
    tok_dev = queries.shape[1]
    inner = queries.shape[2]
    rank = adapter_in.shape[1]
    groups = lax.axis_size("sp")
    tokens = tok_dev * groups
    heads = inner // HD
    head_share = heads // groups
    positions = jnp.arange(tokens, dtype=jnp.int32)
    segment = segment_ids(clip_count[0], clip_lengths[0], positions)
    segment_mine = lax.dynamic_slice_in_dim(segment, lax.axis_index("sp") * tok_dev, tok_dev)
    live = (segment_mine < MAX_CLIPS).astype(out_grad.dtype)
    grad_live = out_grad[0] * live[:, None]
    block = math.gcd(512, tokens)
    blocks = tokens // block

    def attend_head(query_head, key_head, value_head):

        def one_block(pair):
            query_block, segment_block = pair
            scores = lax.dot_general(
                query_block, key_head, (((1,), (1,)), ((), ())), preferred_element_type=jnp.float32
            ) * HD ** (-0.5)
            allowed = segment_block[:, None] == segment[None, :]
            highest = jnp.max(jnp.where(allowed, scores, -jnp.inf), axis=1, keepdims=True)
            exponent = jnp.exp(jnp.where(allowed, scores - highest, -jnp.inf))
            row_total = jnp.sum(exponent, axis=1, keepdims=True)
            weights = exponent.astype(jnp.bfloat16)
            mixed = jnp.dot(weights, value_head, preferred_element_type=jnp.float32) / row_total
            return mixed.astype(jnp.bfloat16)

        result = lax.map(
            one_block, (query_head.reshape(blocks, block, HD), segment.reshape(blocks, block))
        )
        return result.reshape(tokens, HD)

    query_split = queries.reshape(tok_dev, groups, head_share, HD)
    key_split = key_rows.reshape(tok_dev, groups, head_share, HD)
    value_split = values.reshape(tok_dev, groups, head_share, HD)
    query_part = lax.all_to_all(query_split, "sp", split_axis=1, concat_axis=0, tiled=True)
    key_part = lax.all_to_all(key_split, "sp", split_axis=1, concat_axis=0, tiled=True)
    value_part = lax.all_to_all(value_split, "sp", split_axis=1, concat_axis=0, tiled=True)
    per_head = jax.vmap(attend_head, in_axes=1, out_axes=1)
    mixed = per_head(query_part[:, 0], key_part[:, 0], value_part[:, 0])[:, None]
    returned = lax.all_to_all(mixed, "sp", split_axis=0, concat_axis=1, tiled=True)
    attended = returned.reshape(tok_dev, inner)
    inner_all, outer_all = gather_packed(
        (adapter_in.astype(jnp.bfloat16), adapter_out.astype(jnp.bfloat16)), "sp", (0, 0)
    )
    adapted = (
        jnp.dot(attended, inner_all, preferred_element_type=jnp.float32) * inner ** (-0.5)
    ).astype(jnp.bfloat16)
    slopes = (
        lax.dot_general(
            grad_live, outer_all, (((1,), (1,)), ((), ())), preferred_element_type=jnp.float32
        )
        * rank ** (-0.5)
    ).astype(jnp.bfloat16)
    term_in = contract_rows(attended, slopes) * inner ** (-0.5)
    term_out = contract_rows(adapted, grad_live) * rank ** (-0.5)
    grad_in, grad_out = sum_packed((term_in, term_out), "sp", (0, 0))
    grad_in, grad_out = packed_total((grad_in, grad_out), "rep")
    momentum_in, variance_in, update_in = adamw(adapter_in, grad_in, moment_in, square_in)
    momentum_out, variance_out, update_out = adamw(adapter_out, grad_out, moment_out, square_out)
    return (momentum_in, variance_in, update_in, momentum_out, variance_out, update_out)


def solution(mesh):
    placed = (
        P("rep", "sp", None),
        P("rep", "sp", None),
        P("rep", "sp", None),
        P("rep", "sp", None),
        P("rep"),
        P("rep", None),
        P("sp", None),
        P("sp", None),
        P("sp", None),
        P("sp", None),
        P("sp", None),
        P("sp", None),
    )
    return jax.shard_map(
        per_device,
        mesh=mesh,
        in_specs=placed,
        out_specs=(
            P("sp", None),
            P("sp", None),
            P("sp", None),
            P("sp", None),
            P("sp", None),
            P("sp", None),
        ),
        check_vma=False,
    )
```

profile of v0, /device:TPU:8, one launch (start us, length us, event | category | flops | bytes accessed | tf_op | source)
XLA Modules:
  0.0 250.4 jit_solution(16553010181526871349)
XLA Ops:
  7.2 1.4 copy.51
  8.5 1.1 copy.42
  9.7 9.4 %all-to-all-start = ((bf16[192,16,1,128]{3,0,2,1:T(8,128)(2,1)}), bf16[192,16,1,128]{3,0,2,1:T(8,128)(2,1)S(1)}, u32[]{:S(2)}, u32[]{:S(2)}) async-start(bf16[192,16,1,128]{3,0,2,1:T(8,128)(2,1)} %copy.42), calls=%async_computation | async-start | bytes 1572864 | tf_op jit(solution)/shard_map/all_to_all | solution.py:163
  19.2 1.1 copy.43
  20.3 11.0 %all-to-all-done = bf16[192,16,1,128]{3,0,2,1:T(8,128)(2,1)S(1)} async-done(((bf16[192,16,1,128]{3,0,2,1:T(8,128)(2,1)}), bf16[192,16,1,128]{3,0,2,1:T(8,128)(2,1)S(1)}, u32[]{:S(2)}, u32[]{:S(2)}) %all-to-all-start) | async-done | bytes 786464 | tf_op jit(solution)/shard_map/all_to_all | solution.py:163
  31.3 5.0 %all-to-all-start.1 = ((bf16[192,16,1,128]{3,0,2,1:T(8,128)(2,1)}), bf16[192,16,1,128]{3,0,2,1:T(8,128)(2,1)S(1)}, u32[]{:S(2)}, u32[]{:S(2)}) async-start(bf16[192,16,1,128]{3,0,2,1:T(8,128)(2,1)} %copy.43), calls=%async_computation.1 | async-start | bytes 1572864 | tf_op jit(solution)/shard_map/all_to_all | solution.py:164
  36.5 1.1 copy.44
  37.6 11.0 %all-to-all-done.1 = bf16[192,16,1,128]{3,0,2,1:T(8,128)(2,1)S(1)} async-done(((bf16[192,16,1,128]{3,0,2,1:T(8,128)(2,1)}), bf16[192,16,1,128]{3,0,2,1:T(8,128)(2,1)S(1)}, u32[]{:S(2)}, u32[]{:S(2)}) %all-to-all-start.1) | async-done | bytes 786464 | tf_op jit(solution)/shard_map/all_to_all | solution.py:164
  48.7 5.0 %all-to-all-start.2 = ((bf16[192,16,1,128]{3,0,2,1:T(8,128)(2,1)}), bf16[192,16,1,128]{3,0,2,1:T(8,128)(2,1)S(1)}, u32[]{:S(2)}, u32[]{:S(2)}) async-start(bf16[192,16,1,128]{3,0,2,1:T(8,128)(2,1)} %copy.44), calls=%async_computation.2 | async-start | bytes 1572864 | tf_op jit(solution)/shard_map/all_to_all | solution.py:165
  55.4 10.5 %all-to-all-done.2 = bf16[192,16,1,128]{3,0,2,1:T(8,128)(2,1)S(1)} async-done(((bf16[192,16,1,128]{3,0,2,1:T(8,128)(2,1)}), bf16[192,16,1,128]{3,0,2,1:T(8,128)(2,1)S(1)}, u32[]{:S(2)}, u32[]{:S(2)}) %all-to-all-start.2) | async-done | bytes 786464 | tf_op jit(solution)/shard_map/all_to_all | solution.py:165
  66.0 31.9 %while.10 = (s32[]{:T(128)}, bf16[6,1,512,128]{3,2,1,0:T(8,128)(2,1)S(1)}, s32[6,512]{1,0:T(8,128)S(1)}, s32[3072]{0:T(1024)S(1)}, bf16[6,1,512,128]{3,2,1,0:T(8...) while((s32[]{:T(128)}, ...), condition=%wide.region_5.6_spmd, body=%wide.region_2.5_spmd.sunk | while | flops 827456512 | bytes 20766816 | solution.py:155
  66.0 1.2 fusion.65
  67.2 1.9 fusion.66
  69.0 2.2 fusion.67
  71.3 1.2 fusion.65
  72.5 1.9 fusion.66
  74.3 2.2 fusion.67
  76.6 1.2 fusion.65
  77.8 1.9 fusion.66
  79.7 2.2 fusion.67
  81.9 1.2 fusion.65
  83.1 1.9 fusion.66
  85.0 2.2 fusion.67
  87.2 1.2 fusion.65
  88.4 1.9 fusion.66
  90.3 2.2 fusion.67
  92.5 1.2 fusion.65
  93.7 1.9 fusion.66
  95.6 2.2 fusion.67
  98.3 1.2 reduce.5
  99.6 1.1 reshape.153
  100.7 5.0 %all-to-all-start.3 = ((bf16[16,2,12288]{2,1,0:T(2,128)(2,1)}), bf16[16,2,12288]{2,1,0:T(2,128)(2,1)S(1)}, u32[]{:S(2)}, u32[]{:S(2)}) async-start(bf16[16,2,12288]{2,1,0:T(2,128)(2,1)} %reshape.153), calls=%async_computation.3 | async-start | bytes 1572864 | tf_op jit(solution)/shard_map/all_to_all | solution.py:168
  105.8 1.7 reshape.152
  107.8 1.2 reshape_reshape.12
  109.1 8.9 %all-to-all-done.3 = bf16[16,2,12288]{2,1,0:T(2,128)(2,1)S(1)} async-done(((bf16[16,2,12288]{2,1,0:T(2,128)(2,1)}), bf16[16,2,12288]{2,1,0:T(2,128)(2,1)S(1)}, u32[]{:S(2)}, u32[]{:S(2)}) %all-to-all-start.3) | async-done | bytes 786464 | tf_op jit(solution)/shard_map/all_to_all | solution.py:168
  118.0 0.7 reshape.154
  119.4 2.0 convolution_multiply_fusion
  121.4 1.4 reshape_reshape.15
  122.8 2.9 %convolution_multiply_fusion.1 = f32[2048,128]{1,0:T(8,128)S(1)} fusion(bf16[128,3072]{1,0:T(8,128)(2,1)} %reshape_reshape.12, bf16[1,192,3072]{2,1,0:T(8,128)(2,1)} %param.17, bf16[24,8,16,128]{3,2,1,0:T(8,128)(2,1)S(1)} %bitcast.105, bf16[192]{0:T(256)(128)(2,1)S(1)} %compare_convert_fusion), kind=kOutput, calls=%fused_computation.22 | convolution fusion | flops 252559360 | bytes 3801472 | tf_op jit(solution)/shard_map/dot_general | solution.py:106
  125.8 1.2 reshape_reshape.13
  126.9 1.9 pad_maximum_fusion
  128.8 1.7 reshape.149
  130.6 68.7 %reduce-scatter.2.cloned.1.call-done = f32[320,128]{1,0:T(8,128)} async-done(((f32[5120,128]{1,0:T(8,128)}), f32[320,128]{1,0:T(8,128)}) %reduce-scatter.2.cloned.1.call-update) | async-done | bytes 163856 | tf_op jit(solution)/shard_map/reduce_scatter | solution.py:44
  199.2 0.9 slice_bitcast_fusion
  200.1 0.8 slice_bitcast_fusion.1
  201.0 24.9 %all_to_all.75 = f32[32,1,1280]{2,1,0:T(1,128)S(1)} all-to-all(f32[32,1,1280]{2,1,0:T(1,128)S(1)} %bitcast.119), channel_id=1, replica_groups=mesh['rep'=32,'sp'=16] {'rep'}, dimensions={0} | all-to-all | bytes 327680 | tf_op jit(solution)/shard_map/all_to_all | solution.py:72
  226.1 15.9 %all_to_all.76 = f32[32,1,1280]{2,1,0:T(1,128)S(1)} all-to-all(f32[32,1,1280]{2,1,0:T(1,128)S(1)} %broadcast_in_dim.21), channel_id=1, replica_groups=mesh['rep'=32,'sp'=16] {'rep'}, dimensions={0} | all-to-all | bytes 327680 | tf_op jit(solution)/shard_map/all_to_all | solution.py:61
  242.1 0.7 multiply_add_fusion
  (55 shorter events, 3.9 us)
Async XLA Ops:
  7.2 11.9 %copy-start = (bf16[1,192,2048]{2,1,0:T(8,128)(2,1)S(1)}, bf16[1,192,2048]{2,1,0:T(8,128)(2,1)}, u32[]{:S(2)}) copy-start(bf16[1,192,2048]{2,1,0:T(8,128)(2,1)} %param.15) | copy-start | bytes 2359300
  9.7 26.7 %copy-start.1 = (bf16[1,192,2048]{2,1,0:T(8,128)(2,1)S(1)}, bf16[1,192,2048]{2,1,0:T(8,128)(2,1)}, u32[]{:S(2)}) copy-start(bf16[1,192,2048]{2,1,0:T(8,128)(2,1)} %param.16) | copy-start | bytes 2359300
  9.7 21.7 %all-to-all-start = ((bf16[192,16,1,128]{3,0,2,1:T(8,128)(2,1)}), bf16[192,16,1,128]{3,0,2,1:T(8,128)(2,1)S(1)}, u32[]{:S(2)}, u32[]{:S(2)}) async-start(bf16[192,16,1,128]{3,0,2,1:T(8,128)(2,1)} %copy.42), calls=%async_computation | async-start | bytes 1572864 | tf_op jit(solution)/shard_map/all_to_all | solution.py:163
  20.3 33.4 %copy-start.2 = (f32[8,3072]{1,0:T(8,128)S(1)}, f32[8,3072]{1,0:T(8,128)}, u32[]{:S(2)}) copy-start(f32[8,3072]{1,0:T(8,128)} %param.21) | copy-start | bytes 294916
  20.3 33.5 %copy-start.3 = (f32[128,128]{1,0:T(8,128)S(1)}, f32[128,128]{1,0:T(8,128)}, u32[]{:S(2)}) copy-start(f32[128,128]{1,0:T(8,128)} %param.20) | copy-start | bytes 196612
  20.3 34.8 %copy-start.9 = (s32[1,3]{1,0:T(1,128)S(1)}, s32[1,3]{1,0:T(1,128)}, u32[]{:S(2)}) copy-start(s32[1,3]{1,0:T(1,128)} %param.19) | copy-start | bytes 40
  31.3 17.3 %all-to-all-start.1 = ((bf16[192,16,1,128]{3,0,2,1:T(8,128)(2,1)}), bf16[192,16,1,128]{3,0,2,1:T(8,128)(2,1)S(1)}, u32[]{:S(2)}, u32[]{:S(2)}) async-start(bf16[192,16,1,128]{3,0,2,1:T(8,128)(2,1)} %copy.43), calls=%async_computation.1 | async-start | bytes 1572864 | tf_op jit(solution)/shard_map/all_to_all | solution.py:164
  48.7 17.3 %all-to-all-start.2 = ((bf16[192,16,1,128]{3,0,2,1:T(8,128)(2,1)}), bf16[192,16,1,128]{3,0,2,1:T(8,128)(2,1)S(1)}, u32[]{:S(2)}, u32[]{:S(2)}) async-start(bf16[192,16,1,128]{3,0,2,1:T(8,128)(2,1)} %copy.44), calls=%async_computation.2 | async-start | bytes 1572864 | tf_op jit(solution)/shard_map/all_to_all | solution.py:165
  53.7 52.1 %all-gather.3.cloned.1.call-start = ((), (), s32[]{:S(2)}) async-start(), calls=%async_computation.8 | async-start | bytes 1392640 | tf_op jit(solution)/shard_map/all_gather | solution.py:24
  100.7 17.3 %all-to-all-start.3 = ((bf16[16,2,12288]{2,1,0:T(2,128)(2,1)}), bf16[16,2,12288]{2,1,0:T(2,128)(2,1)S(1)}, u32[]{:S(2)}, u32[]{:S(2)}) async-start(bf16[16,2,12288]{2,1,0:T(2,128)(2,1)} %reshape.153), calls=%async_computation.3 | async-start | bytes 1572864 | tf_op jit(solution)/shard_map/all_to_all | solution.py:168
  105.7 93.6 %reduce-scatter.2.cloned.1.call-start = ((), (), s32[]{:S(2)}) async-start(), calls=%async_computation.7 | async-start | bytes 2785280 | tf_op jit(solution)/shard_map/reduce_scatter | solution.py:44
  130.5 111.6 %copy-start.5 = (f32[8,3072]{1,0:T(8,128)S(1)}, f32[8,3072]{1,0:T(8,128)}, u32[]{:S(2)}) copy-start(f32[8,3072]{1,0:T(8,128)} %param.25) | copy-start | bytes 294916
  130.5 111.6 %copy-start.6 = (f32[8,3072]{1,0:T(8,128)S(1)}, f32[8,3072]{1,0:T(8,128)}, u32[]{:S(2)}) copy-start(f32[8,3072]{1,0:T(8,128)} %param.24) | copy-start | bytes 294916
  130.5 112.3 %copy-start.4 = (f32[128,128]{1,0:T(8,128)S(1)}, f32[128,128]{1,0:T(8,128)}, u32[]{:S(2)}) copy-start(f32[128,128]{1,0:T(8,128)} %param.20) | copy-start | bytes 196612
  130.5 112.3 %copy-start.7 = (f32[128,128]{1,0:T(8,128)S(1)}, f32[128,128]{1,0:T(8,128)}, u32[]{:S(2)}) copy-start(f32[128,128]{1,0:T(8,128)} %param.23) | copy-start | bytes 196612
  130.5 112.3 %copy-start.8 = (f32[128,128]{1,0:T(8,128)S(1)}, f32[128,128]{1,0:T(8,128)}, u32[]{:S(2)}) copy-start(f32[128,128]{1,0:T(8,128)} %param.22) | copy-start | bytes 196612
Sparse Core Ops, SparseCore 0:
  57.2 37.8 all-gather.2
  130.7 68.4 reduce-scatter.1
where the time goes:
time: 251 us; the launch traced here: 250 us
  waiting for transfers between devices  110 us (44%)
  blocking collectives  40.9 us (16%)
  matrix products  25.5 us (10%)
  starting transfers between devices  24.5 us (10%)
  local copies, waits for them, and re-layouts  17.5 us (7%)
  other arithmetic  16.8 us (7%)
  between operations  14.9 us (6%)
    reduce_scatter x1, waiting for transfers between devices, sum_packed(): lax.psum_scatter(lines, axis, tiled=True).reshape(-1)  68.7 us
    all_to_all x1, blocking collectives, summed_on_arrival(): lax.all_to_all(blocks, axis, split_axis=0, concat_axis=0, tiled=True)  24.9 us
    all_to_all x1, blocking collectives, sent_to_all(): lax.all_to_all(jnp.broadcast_to(array[None], (peers, *array.shape)), axis...  15.9 us
    dot_general x6, matrix products, one_block(): jnp.dot(weights, value_head, preferred_element_type=jnp.float32) / row_total  13.4 us
    reduce_sum x6, other arithmetic, one_block(): row_total = jnp.sum(exponent, axis=1, keepdims=True)  11.1 us
    all_to_all x1, waiting for transfers between devices, per_device(): lax.all_to_all(query_split, 'sp', split_axis=1, concat_axis=0, tiled=True)  11 us
    all_to_all x1, waiting for transfers between devices, per_device(): lax.all_to_all(key_split, 'sp', split_axis=1, concat_axis=0, tiled=True)  11 us
    all_to_all x1, waiting for transfers between devices, per_device(): lax.all_to_all(value_split, 'sp', split_axis=1, concat_axis=0, tiled=True)  10.5 us
  transfers between devices with their start and end apart: 6, of which 5 were waited for; matrix products, arithmetic and copies ran while one was open for 16% of the time, Pallas kernels for 0%

commit v1 on v0

--- a/solution.py
+++ b/solution.py
@@ -11,6 +11,13 @@
 adam_steps = 100.0
 adam_epsilon = 1e-08
 decay_rate = 0.1
+
+
+def stacked_exchange(x, mesh_axis, split, join):
+    size = lax.axis_size(mesh_axis)
+    blocks = jnp.stack(jnp.split(x, size, axis=split), axis=0)
+    blocks = lax.all_to_all(blocks, mesh_axis, split_axis=0, concat_axis=0)
+    return jnp.concatenate(blocks, axis=join)
 
 
 def laid_out(blocks, dim):
@@ -165,7 +172,7 @@
     value_part = lax.all_to_all(value_split, "sp", split_axis=1, concat_axis=0, tiled=True)
     per_head = jax.vmap(attend_head, in_axes=1, out_axes=1)
     mixed = per_head(query_part[:, 0], key_part[:, 0], value_part[:, 0])[:, None]
-    returned = lax.all_to_all(mixed, "sp", split_axis=0, concat_axis=1, tiled=True)
+    returned = stacked_exchange(mixed, "sp", 0, 1)
     attended = returned.reshape(tok_dev, inner)
     inner_all, outer_all = gather_packed(
         (adapter_in.astype(jnp.bfloat16), adapter_out.astype(jnp.bfloat16)), "sp", (0, 0)

time: 251 us -> 257 us (1.024)
  local copies, waits for them, and re-layouts: 17.5 us -> 25.7 us
    unnamed x27 -> x41, local copies, waits for them, and re-layouts: 3.66 us -> 11 us
  transfers between devices with their start and end apart: 6 -> 6, of which waited for: 5 -> 5; matrix products, arithmetic and copies ran while one was open for 16% -> 19% of each run, Pallas kernels for 0% -> 0%
where the time goes in v1:
time: 257 us
  waiting for transfers between devices  109 us (42%)
  blocking collectives  41.1 us (16%)
  local copies, waits for them, and re-layouts  25.7 us (10%)
  matrix products  25.5 us (10%)
  starting transfers between devices  24.5 us (10%)
  other arithmetic  15.6 us (6%)
  between operations  14.9 us (6%)
    reduce_scatter x1, waiting for transfers between devices, sum_packed(): lax.psum_scatter(lines, axis, tiled=True).reshape(-1)  68.4 us
    all_to_all x1, blocking collectives, summed_on_arrival(): lax.all_to_all(blocks, axis, split_axis=0, concat_axis=0, tiled=True)  25.1 us
    all_to_all x1, blocking collectives, sent_to_all(): lax.all_to_all(jnp.broadcast_to(array[None], (peers, *array.shape)), axis...  15.9 us
    dot_general x6, matrix products, one_block(): jnp.dot(weights, value_head, preferred_element_type=jnp.float32) / row_total  13.4 us
    reduce_sum x6, other arithmetic, one_block(): row_total = jnp.sum(exponent, axis=1, keepdims=True)  11.1 us
    all_to_all x1, waiting for transfers between devices, per_device(): lax.all_to_all(key_split, 'sp', split_axis=1, concat_axis=0, tiled=True)  11 us
    all_to_all x1, waiting for transfers between devices, per_device(): lax.all_to_all(query_split, 'sp', split_axis=1, concat_axis=0, tiled=True)  11 us
    unnamed x41, local copies, waits for them, and re-layouts  11 us
  transfers between devices with their start and end apart: 6, of which 5 were waited for; matrix products, arithmetic and copies ran while one was open for 19% of the time, Pallas kernels for 0%

profile of v1, /device:TPU:8, one launch (start us, length us, event | category | flops | bytes accessed | tf_op | source)
XLA Modules:
  0.0 256.7 jit_solution(5649822319099927018)
XLA Ops:
  7.2 1.4 copy.62
  8.5 1.1 copy.55
  9.7 9.4 %all-to-all-start = ((bf16[192,16,1,128]{3,0,2,1:T(8,128)(2,1)}), bf16[192,16,1,128]{3,0,2,1:T(8,128)(2,1)S(1)}, u32[]{:S(2)}, u32[]{:S(2)}) async-start(bf16[192,16,1,128]{3,0,2,1:T(8,128)(2,1)} %copy.55), calls=%async_computation | async-start | bytes 1572864 | tf_op jit(solution)/shard_map/all_to_all | solution.py:170
  19.2 1.1 copy.56
  20.3 11.0 %all-to-all-done = bf16[192,16,1,128]{3,0,2,1:T(8,128)(2,1)S(1)} async-done(((bf16[192,16,1,128]{3,0,2,1:T(8,128)(2,1)}), bf16[192,16,1,128]{3,0,2,1:T(8,128)(2,1)S(1)}, u32[]{:S(2)}, u32[]{:S(2)}) %all-to-all-start) | async-done | bytes 786464 | tf_op jit(solution)/shard_map/all_to_all | solution.py:170
  31.3 5.0 %all-to-all-start.1 = ((bf16[192,16,1,128]{3,0,2,1:T(8,128)(2,1)}), bf16[192,16,1,128]{3,0,2,1:T(8,128)(2,1)S(1)}, u32[]{:S(2)}, u32[]{:S(2)}) async-start(bf16[192,16,1,128]{3,0,2,1:T(8,128)(2,1)} %copy.56), calls=%async_computation.1 | async-start | bytes 1572864 | tf_op jit(solution)/shard_map/all_to_all | solution.py:171
  36.5 1.1 copy.57
  37.6 11.0 %all-to-all-done.1 = bf16[192,16,1,128]{3,0,2,1:T(8,128)(2,1)S(1)} async-done(((bf16[192,16,1,128]{3,0,2,1:T(8,128)(2,1)}), bf16[192,16,1,128]{3,0,2,1:T(8,128)(2,1)S(1)}, u32[]{:S(2)}, u32[]{:S(2)}) %all-to-all-start.1) | async-done | bytes 786464 | tf_op jit(solution)/shard_map/all_to_all | solution.py:171
  48.7 5.0 %all-to-all-start.2 = ((bf16[192,16,1,128]{3,0,2,1:T(8,128)(2,1)}), bf16[192,16,1,128]{3,0,2,1:T(8,128)(2,1)S(1)}, u32[]{:S(2)}, u32[]{:S(2)}) async-start(bf16[192,16,1,128]{3,0,2,1:T(8,128)(2,1)} %copy.57), calls=%async_computation.2 | async-start | bytes 1572864 | tf_op jit(solution)/shard_map/all_to_all | solution.py:172
  53.8 0.6 pad_maximum_fusion.2
  55.4 10.5 %all-to-all-done.2 = bf16[192,16,1,128]{3,0,2,1:T(8,128)(2,1)S(1)} async-done(((bf16[192,16,1,128]{3,0,2,1:T(8,128)(2,1)}), bf16[192,16,1,128]{3,0,2,1:T(8,128)(2,1)S(1)}, u32[]{:S(2)}, u32[]{:S(2)}) %all-to-all-start.2) | async-done | bytes 786464 | tf_op jit(solution)/shard_map/all_to_all | solution.py:172
  66.0 31.9 %while.10 = (s32[]{:T(128)}, bf16[6,1,512,128]{3,2,1,0:T(8,128)(2,1)S(1)}, s32[6,512]{1,0:T(8,128)S(1)}, s32[3072]{0:T(1024)S(1)}, bf16[6,1,512,128]{3,2,1,0:T(8...) while((s32[]{:T(128)}, ...), condition=%wide.region_5.6_spmd, body=%wide.region_2.5_spmd.sunk | while | flops 827456512 | bytes 20766816 | solution.py:162
  66.0 1.2 fusion.81
  67.2 1.9 fusion.82
  69.0 2.2 fusion.83
  71.3 1.2 fusion.81
  72.5 1.9 fusion.82
  74.3 2.2 fusion.83
  76.6 1.2 fusion.81
  77.8 1.9 fusion.82
  79.7 2.2 fusion.83
  81.9 1.2 fusion.81
  83.1 1.9 fusion.82
  85.0 2.2 fusion.83
  87.2 1.2 fusion.81
  88.4 1.9 fusion.82
  90.3 2.2 fusion.83
  92.5 1.2 fusion.81
  93.7 1.9 fusion.82
  95.6 2.2 fusion.83
  107.7 5.0 %all-to-all-start.3 = ((bf16[16,192,1,1,128]{4,1,3,2,0:T(8,128)(2,1)}), bf16[16,192,1,1,128]{4,1,3,2,0:T(8,128)(2,1)S(1)}, u32[]{:S(2)}, u32[]{:S(2)}) async-start(bf16[16,192,1,1,128]{4,1,3,2,0:T(8,128)(2,1)} %fusion.49), calls=%async_computation.3 | async-start | bytes 1572864 | tf_op jit(solution)/shard_map/all_to_all | solution.py:19
  112.9 1.7 reshape.151
  114.7 1.2 reshape_reshape.16
  115.9 1.0 reshape_reshape.18
  117.0 8.1 %all-to-all-done.3 = bf16[16,192,1,1,128]{4,1,3,2,0:T(8,128)(2,1)S(1)} async-done(((bf16[16,192,1,1,128]{4,1,3,2,0:T(8,128)(2,1)}), bf16[16,192,1,1,128]{4,1,3,2,0:T(8,128)(2,1)S(1)}, u32[]{:S(2)}, u32[]{:S(2)}) %all-to-all-start.3) | async-done | bytes 786464 | tf_op jit(solution)/shard_map/all_to_all | solution.py:19
  125.6 3.0 %convolution_multiply_fusion.1 = f32[2048,128]{1,0:T(8,128)S(1)} fusion(bf16[128,3072]{1,0:T(8,128)(2,1)} %reshape_reshape.16, bf16[1,192,3072]{2,1,0:T(8,128)(2,1)} %param.17, bf16[24,8,16,128]{3,2,1,0:T(8,128)(2,1)S(1)} %bitcast.166, bf16[192]{0:T(256)(128)(2,1)S(1)} %compare_convert_fusion), kind=kOutput, calls=%fused_computation.22 | convolution fusion | flops 252559360 | bytes 3801472 | tf_op jit(solution)/shard_map/dot_general | solution.py:113
  128.6 1.2 reshape_reshape.17
  129.8 2.0 convolution_multiply_fusion
  131.8 1.4 reshape_reshape.19
  133.2 1.9 pad_maximum_fusion
  135.1 1.7 reshape.148
  136.9 68.4 %reduce-scatter.2.cloned.1.call-done = f32[320,128]{1,0:T(8,128)} async-done(((f32[5120,128]{1,0:T(8,128)}), f32[320,128]{1,0:T(8,128)}) %reduce-scatter.2.cloned.1.call-update) | async-done | bytes 163856 | tf_op jit(solution)/shard_map/reduce_scatter | solution.py:51
  205.3 0.9 slice_bitcast_fusion
  206.2 0.8 slice_bitcast_fusion.1
  207.1 25.1 %all_to_all.65 = f32[32,1,1280]{2,1,0:T(1,128)S(1)} all-to-all(f32[32,1,1280]{2,1,0:T(1,128)S(1)} %bitcast.196), channel_id=1, replica_groups=mesh['rep'=32,'sp'=16] {'rep'}, dimensions={0} | all-to-all | bytes 327680 | tf_op jit(solution)/shard_map/all_to_all | solution.py:79
  232.4 15.9 %all_to_all.66 = f32[32,1,1280]{2,1,0:T(1,128)S(1)} all-to-all(f32[32,1,1280]{2,1,0:T(1,128)S(1)} %broadcast_in_dim.21), channel_id=1, replica_groups=mesh['rep'=32,'sp'=16] {'rep'}, dimensions={0} | all-to-all | bytes 327680 | tf_op jit(solution)/shard_map/all_to_all | solution.py:68
  248.4 0.7 multiply_add_fusion
  249.2 0.7 multiply_add_fusion.2
  (68 shorter events, 11.6 us)
Async XLA Ops:
  7.2 11.9 %copy-start.1 = (bf16[1,192,2048]{2,1,0:T(8,128)(2,1)S(1)}, bf16[1,192,2048]{2,1,0:T(8,128)(2,1)}, u32[]{:S(2)}) copy-start(bf16[1,192,2048]{2,1,0:T(8,128)(2,1)} %param.15) | copy-start | bytes 2359300
  9.7 26.7 %copy-start.2 = (bf16[1,192,2048]{2,1,0:T(8,128)(2,1)S(1)}, bf16[1,192,2048]{2,1,0:T(8,128)(2,1)}, u32[]{:S(2)}) copy-start(bf16[1,192,2048]{2,1,0:T(8,128)(2,1)} %param.16) | copy-start | bytes 2359300
  9.7 21.7 %all-to-all-start = ((bf16[192,16,1,128]{3,0,2,1:T(8,128)(2,1)}), bf16[192,16,1,128]{3,0,2,1:T(8,128)(2,1)S(1)}, u32[]{:S(2)}, u32[]{:S(2)}) async-start(bf16[192,16,1,128]{3,0,2,1:T(8,128)(2,1)} %copy.55), calls=%async_computation | async-start | bytes 1572864 | tf_op jit(solution)/shard_map/all_to_all | solution.py:170
  20.3 33.4 %copy-start.3 = (f32[8,3072]{1,0:T(8,128)S(1)}, f32[8,3072]{1,0:T(8,128)}, u32[]{:S(2)}) copy-start(f32[8,3072]{1,0:T(8,128)} %param.21) | copy-start | bytes 294916
  20.3 33.5 %copy-start.4 = (f32[128,128]{1,0:T(8,128)S(1)}, f32[128,128]{1,0:T(8,128)}, u32[]{:S(2)}) copy-start(f32[128,128]{1,0:T(8,128)} %param.20) | copy-start | bytes 196612
  20.3 34.8 %copy-start.10 = (s32[1,3]{1,0:T(1,128)S(1)}, s32[1,3]{1,0:T(1,128)}, u32[]{:S(2)}) copy-start(s32[1,3]{1,0:T(1,128)} %param.19) | copy-start | bytes 40
  31.3 17.3 %all-to-all-start.1 = ((bf16[192,16,1,128]{3,0,2,1:T(8,128)(2,1)}), bf16[192,16,1,128]{3,0,2,1:T(8,128)(2,1)S(1)}, u32[]{:S(2)}, u32[]{:S(2)}) async-start(bf16[192,16,1,128]{3,0,2,1:T(8,128)(2,1)} %copy.56), calls=%async_computation.1 | async-start | bytes 1572864 | tf_op jit(solution)/shard_map/all_to_all | solution.py:171
  48.7 17.3 %all-to-all-start.2 = ((bf16[192,16,1,128]{3,0,2,1:T(8,128)(2,1)}), bf16[192,16,1,128]{3,0,2,1:T(8,128)(2,1)S(1)}, u32[]{:S(2)}, u32[]{:S(2)}) async-start(bf16[192,16,1,128]{3,0,2,1:T(8,128)(2,1)} %copy.57), calls=%async_computation.2 | async-start | bytes 1572864 | tf_op jit(solution)/shard_map/all_to_all | solution.py:172
  53.7 59.2 %all-gather.3.cloned.1.call-start = ((), (), s32[]{:S(2)}) async-start(), calls=%async_computation.8 | async-start | bytes 1392640 | tf_op jit(solution)/shard_map/all_gather | solution.py:31
  107.7 17.3 %all-to-all-start.3 = ((bf16[16,192,1,1,128]{4,1,3,2,0:T(8,128)(2,1)}), bf16[16,192,1,1,128]{4,1,3,2,0:T(8,128)(2,1)S(1)}, u32[]{:S(2)}, u32[]{:S(2)}) async-start(bf16[16,192,1,1,128]{4,1,3,2,0:T(8,128)(2,1)} %fusion.49), calls=%async_computation.3 | async-start | bytes 1572864 | tf_op jit(solution)/shard_map/all_to_all | solution.py:19
  112.8 92.6 %reduce-scatter.2.cloned.1.call-start = ((), (), s32[]{:S(2)}) async-start(), calls=%async_computation.7 | async-start | bytes 2785280 | tf_op jit(solution)/shard_map/reduce_scatter | solution.py:51
  125.6 4.2 %copy-start = (bf16[2048,128]{1,0:T(8,128)(2,1)S(1)}, bf16[2048,128]{1,0:T(8,128)(2,1)}, u32[]{:S(2)}) copy-start(bf16[2048,128]{1,0:T(8,128)(2,1)} %reshape_reshape.18) | copy-start | bytes 1572868
  136.8 111.6 %copy-start.6 = (f32[8,3072]{1,0:T(8,128)S(1)}, f32[8,3072]{1,0:T(8,128)}, u32[]{:S(2)}) copy-start(f32[8,3072]{1,0:T(8,128)} %param.25) | copy-start | bytes 294916
  136.8 111.6 %copy-start.7 = (f32[8,3072]{1,0:T(8,128)S(1)}, f32[8,3072]{1,0:T(8,128)}, u32[]{:S(2)}) copy-start(f32[8,3072]{1,0:T(8,128)} %param.24) | copy-start | bytes 294916
  136.8 112.3 %copy-start.5 = (f32[128,128]{1,0:T(8,128)S(1)}, f32[128,128]{1,0:T(8,128)}, u32[]{:S(2)}) copy-start(f32[128,128]{1,0:T(8,128)} %param.20) | copy-start | bytes 196612
  136.8 112.3 %copy-start.8 = (f32[128,128]{1,0:T(8,128)S(1)}, f32[128,128]{1,0:T(8,128)}, u32[]{:S(2)}) copy-start(f32[128,128]{1,0:T(8,128)} %param.23) | copy-start | bytes 196612
  136.8 112.3 %copy-start.9 = (f32[128,128]{1,0:T(8,128)S(1)}, f32[128,128]{1,0:T(8,128)}, u32[]{:S(2)}) copy-start(f32[128,128]{1,0:T(8,128)} %param.22) | copy-start | bytes 196612
Sparse Core Ops, SparseCore 0:
  57.2 37.8 all-gather.2
  137.0 68.2 reduce-scatter.1
